TPU v7x, 32 devices: a whole 2x2x4 slice. The times are simulated.
32 devices in a mesh: grp: 16 (over z, x, core), patch: 2 (over y).
Axes of the slice: x: 2, y: 2, z: 4, core: 2. Of those that a mesh axis runs over, the one named last changes fastest.
Arguments:
- tokens: bfloat16 [12288, 1152], P(('grp', 'patch')), parts along dimension 0, may hold values from -6 to 6
- projection_weight: bfloat16 [1152, 3456], replicated, may hold values from -0.1875 to 0.1875
- shift_term: float32 [1152], replicated, may hold values from -3 to 3
- scale_term: float32 [1152], replicated, may hold values from -3 to 3
- query_gain: float32 [72], replicated, may hold values from 0.1 to 1.9
- key_gain: float32 [72], replicated, may hold values from 0.1 to 1.9
- stale_keys: bfloat16 [12288, 1152], P(('grp', 'patch')), parts along dimension 0, may hold values from -6 to 6
- stale_values: bfloat16 [12288, 1152], P(('grp', 'patch')), parts along dimension 0, may hold values from -6 to 6
- stale_output: bfloat16 [12288, 1152], P(('grp', 'patch')), parts along dimension 0, may hold values from -3 to 3
- refreshed: int32 [768], P('grp'), parts along dimension 0, may hold values from 0 to 1, as said below
Outputs:
- attended: bfloat16 [12288, 1152], P(('grp', 'patch')), parts along dimension 0
There are 16 independent parts, one for each index of `grp`. A program takes and returns all parts, laid end to end along the dimension named above; an argument that names none is the same for every part. Nothing has to cross between parts.
Inputs may be any that keep to these rules, and one draw needn't show every extreme that they name: Exactly 16 of the 48 entries are 1; in every prompt some device has all 16 of its tiles refreshed.
All inputs are finite; a program needn't handle non-finite values.
Results may differ from a plain program's by a relative error of at most 0.0045.
Values may be sent and summed in bfloat16 or wider, within the bound.
No kernel may reach another device: no remote copies, remote signals or barrier semaphores. Data moves between devices by JAX's collectives and lax.ppermute only.
A program may use at most 128 MiB of HBM per device.

v0:
```python
import math
import jax
import jax.numpy as jnp
from jax import lax
from jax.sharding import PartitionSpec as P

H = 16
TILE = 16
epsilon = 1e-06


def modulate(row_block, shift_term, scale_term):
    values = row_block.astype(jnp.float32)
    center = values - jnp.mean(values, axis=-1, keepdims=True)
    spread = jnp.mean(center * center, axis=-1, keepdims=True)
    normed = center / jnp.sqrt(spread + epsilon)
    return (normed * (1.0 + scale_term) + shift_term).astype(jnp.bfloat16)


def head_norm(row_block, gain_vector, head_count):
    values = row_block.astype(jnp.float32).reshape(row_block.shape[0], head_count, -1)
    normed = values / jnp.sqrt(jnp.mean(values * values, axis=-1, keepdims=True) + epsilon)
    return (normed * gain_vector).astype(jnp.bfloat16).reshape(row_block.shape[0], -1)


def block_size(row_total, row_unit):
    multiple = row_total // row_unit
    chosen = 1
    for candidate in range(1, multiple + 1):
        if multiple % candidate == 0 and candidate * row_unit <= 1024:
            chosen = candidate
    return chosen * row_unit


def partial_terms(queries, key_rows, values, head_count):
    query_count = queries.shape[0]
    model_width = queries.shape[1]
    head_size = model_width // head_count
    factor = 1.0 / math.sqrt(head_size)
    query_heads = queries.reshape(query_count, head_count, head_size)
    key_heads = key_rows.reshape(key_rows.shape[0], head_count, head_size)
    value_heads = values.reshape(values.shape[0], head_count, head_size)
    scores = (
        jnp.einsum("qhd,khd->hqk", query_heads, key_heads, preferred_element_type=jnp.float32)
        * factor
    )
    weights = jnp.exp(scores)
    totals = jnp.sum(weights, axis=2).T
    numerator = jnp.einsum(
        "hqk,khd->qhd",
        weights.astype(jnp.bfloat16),
        value_heads,
        preferred_element_type=jnp.float32,
    )
    return (numerator.reshape(query_count, model_width), totals)


def own_terms(every_query, key_rows, values, head_count, row_unit):
    row_total = every_query.shape[0]
    stride = block_size(row_total, row_unit)

    def advance(turn_index, inner_sums):
        offset = turn_index * stride
        query_block = lax.dynamic_slice_in_dim(every_query, offset, stride, 0)
        numerator, totals = partial_terms(query_block, key_rows, values, head_count)
        return (
            lax.dynamic_update_slice_in_dim(inner_sums[0], numerator, offset, 0),
            lax.dynamic_update_slice_in_dim(inner_sums[1], totals, offset, 0),
        )

    starting = (
        jnp.zeros((row_total, key_rows.shape[1]), jnp.float32),
        jnp.zeros((row_total, head_count), jnp.float32),
    )
    return lax.fori_loop(0, row_total // stride, advance, starting)


def attend(queries, own_keys, own_values, head_count):
    query_count = queries.shape[0]
    model_width = queries.shape[1]
    every_query = lax.all_gather(queries, "patch", axis=0, tiled=True)
    numerator, totals = own_terms(every_query, own_keys, own_values, head_count, query_count)
    numerator, totals = (
        lax.psum_scatter(
            numerator.astype(jnp.bfloat16), "patch", scatter_dimension=0, tiled=True
        ).astype(jnp.float32),
        lax.psum_scatter(
            totals.astype(jnp.bfloat16), "patch", scatter_dimension=0, tiled=True
        ).astype(jnp.float32),
    )
    fresh_heads = numerator.reshape(query_count, head_count, -1) / totals[:, :, None]
    return fresh_heads.reshape(query_count, model_width).astype(jnp.bfloat16)


def body(
    tokens,
    projection_weight,
    shift_term,
    scale_term,
    query_gain,
    key_gain,
    stale_keys,
    stale_values,
    stale_output,
    refreshed,
):
    model_width = tokens.shape[1]
    head_count = H
    own_rows = tokens.shape[0]
    own_tiles = own_rows // TILE
    patch_count = lax.axis_size("patch")
    my_index = lax.axis_index("patch")
    share_tiles = own_tiles // 3
    most_tiles = min(own_tiles, share_tiles * patch_count)
    tile_grid = refreshed.reshape(patch_count, own_tiles)
    my_tiles = lax.dynamic_index_in_dim(tile_grid, my_index, 0, keepdims=False)
    picked = jnp.nonzero(my_tiles, size=most_tiles, fill_value=0)[0].astype(jnp.int32)
    token_tiles = tokens.reshape(own_tiles, TILE, model_width)
    chosen = token_tiles[picked].reshape(most_tiles * TILE, model_width)
    hidden = modulate(chosen, shift_term, scale_term)
    projected = jnp.dot(hidden, projection_weight, preferred_element_type=jnp.float32)
    query_new = projected[:, :model_width].astype(jnp.bfloat16)
    key_new = (
        projected[:, model_width : 2 * model_width]
        .astype(jnp.bfloat16)
        .reshape(most_tiles, TILE, model_width)
    )
    value_new = (
        projected[:, 2 * model_width :].astype(jnp.bfloat16).reshape(most_tiles, TILE, model_width)
    )
    position = jnp.maximum(jnp.cumsum(my_tiles) - 1, 0)
    fresh_tile = (my_tiles > 0)[:, None, None]
    keys_all = jnp.where(
        fresh_tile, key_new[position], stale_keys.reshape(own_tiles, TILE, model_width)
    ).reshape(own_rows, model_width)
    values_all = jnp.where(
        fresh_tile, value_new[position], stale_values.reshape(own_tiles, TILE, model_width)
    ).reshape(own_rows, model_width)
    own_keys = head_norm(keys_all, key_gain, head_count)
    queries = head_norm(query_new, query_gain, head_count)
    fresh_rows = attend(queries, own_keys, values_all, head_count)
    fresh_tiles = fresh_rows.reshape(most_tiles, TILE, model_width)
    merged = jnp.where(
        fresh_tile, fresh_tiles[position], stale_output.reshape(own_tiles, TILE, model_width)
    )
    return merged.reshape(own_rows, model_width)


def solution(mesh):
    in_specs = (
        P(("grp", "patch"), None),
        P(),
        P(),
        P(),
        P(),
        P(),
        P(("grp", "patch"), None),
        P(("grp", "patch"), None),
        P(("grp", "patch"), None),
        P("grp"),
    )
    out_specs = P(("grp", "patch"), None)
    return jax.shard_map(body, mesh=mesh, in_specs=in_specs, out_specs=out_specs, check_vma=False)
```

profile of v0, /device:TPU:0, one launch (start us, length us, event | category | flops | bytes accessed | tf_op | source)
XLA Modules:
  0.0 102.9 jit_solution(11285227140400040629)
XLA Ops:
  6.6 0.8 reshape.206
  7.4 0.6 fusion.25
  8.3 0.7 scatter_custom_fusion
  9.1 0.8 fusion.24
  9.9 0.6 gather_fusion
  11.2 0.3 fusion.17
  11.5 5.8 %convolution_convert_fusion = bf16[256,3456]{1,0:T(8,128)(2,1)S(1)} fusion(bf16[256,1152]{1,0:T(8,128)(2,1)S(1)} %fusion.17, bf16[1152,3456]{1,0:T(8,128)(2,1)} %param.11), kind=kOutput, calls=%fused_computation.10 | convolution fusion | flops 2039316480 | bytes 10321920 | tf_op jit(solution)/shard_map/dot_general | solution.py:121
  17.3 1.2 %copy-done.2 = bf16[256,3456]{1,0:T(8,128)(2,1)} copy-done((bf16[256,3456]{1,0:T(8,128)(2,1)}, bf16[256,3456]{1,0:T(8,128)(2,1)S(1)}, u32[]{:S(2)}) %copy-start.2) | copy-done | bytes 1769496
  18.6 0.4 copy.40
  19.2 0.4 copy.41
  19.8 2.1 %fusion.12 = bf16[256,1152]{1,0:T(8,128)(2,1)} fusion(f32[256,1152]{1,0:T(8,128)S(1)} %copy.41, f32[1152]{0:T(1024)S(1)} %mul.54, bf16[256,3456]{1,0:T(8,128)(2,1)} %copy-done.2), kind=kLoop, calls=%fused_computation.19 | loop fusion | flops 1179648 | bytes 2363904 | tf_op jit(solution)/shard_map/convert_element_type | solution.py:23
  22.0 1.3 %fusion.30 = (bf16[256,1152]{1,0:T(8,128)(2,1)S(1)}, bf16[256,1152]{1,0:T(8,128)(2,1)S(1)}) fusion(bf16[256,3456]{1,0:T(8,128)(2,1)} %copy-done.2), kind=kLoop, calls=%fused_computation.60 | loop fusion | bytes 2359296 | tf_op jit(solution)/shard_map/slice | solution.py:129
  23.6 0.7 gather_fusion.2
  24.3 2.6 %fusion.19 = f32[384,1152]{1,0:T(8,128)} fusion(bf16[384,1152]{1,0:T(8,128)(2,1)} %param.16, bf16[24,16,1152]{2,1,0:T(8,128)(2,1)S(1)} %gather_fusion.2, pred[384]{0:T(512)(128)(4,1)S(1)} %broadcast_in_dim.29), kind=kLoop, calls=%fused_computation.31 | loop fusion | flops 884736 | bytes 3539328 | tf_op jit(solution)/shard_map/reshape | solution.py:21
  26.9 2.2 %copy.43 = f32[384,1152]{0,1:T(8,128)S(1)} copy(f32[384,1152]{1,0:T(8,128)} %fusion.19) | data formatting | bytes 3538944 | tf_op jit(solution)/shard_map/reshape | solution.py:21
  29.1 1.6 %gather_fusion.1 = bf16[24,16,1152]{2,1,0:T(8,128)(2,1)} fusion(bf16[16,16,1152]{2,1,0:T(8,128)(2,1)S(1)} %bitcast.50, s32[1024]{0:T(1024)S(1)} %pad_clamp_fusion), kind=kCustom, calls=%fused_computation.1 | custom fusion | bytes 1769568 | tf_op jit(solution)/shard_map/gather | solution.py:137
  30.7 4.7 %gather.20 = bf16[384,16,72]{2,1,0:T(8,128)(2,1)} reshape(bf16[24,16,1152]{2,1,0:T(8,128)(2,1)} %gather_fusion.1) | data formatting | bytes 1769472 | tf_op jit(solution)/shard_map/gather | solution.py:137
  35.4 1.7 %copy.38 = bf16[384,1152]{0,1:T(8,128)(2,1)S(1)} copy(bf16[384,1152]{1,0:T(8,128)(2,1)} %param.17) | data formatting | bytes 1769472 | tf_op args[7]
  37.1 2.0 %copy.39 = bf16[384,16,72]{2,1,0:T(8,128)(2,1)} copy(bf16[384,16,72]{0,2,1:T(8,128)(2,1)S(1)} %bitcast.52) | data formatting | bytes 1769472 | tf_op jit(solution)/shard_map/reshape | solution.py:137
  39.3 1.2 %copy-done.1 = bf16[384,16,72]{2,1,0:T(8,128)(2,1)S(1)} copy-done((bf16[384,16,72]{2,1,0:T(8,128)(2,1)S(1)}, bf16[384,16,72]{2,1,0:T(8,128)(2,1)}, u32[]{:S(2)}) %copy-start.1) | copy-done | bytes 884760
  40.5 3.3 %broadcast_select_fusion = bf16[384,16,72]{2,1,0:T(8,128)(2,1)} fusion(bf16[384,16,72]{2,1,0:T(8,128)(2,1)S(1)} %copy-done.1, bf16[384,16,72]{2,1,0:T(8,128)(2,1)} %copy.39, pred[384]{0:T(512)(128)(4,1)S(1)} %broadcast_in_dim.29), kind=kLoop, calls=%fused_computation.14 | loop fusion | flops 442368 | bytes 2654592 | tf_op jit(solution)/shard_map/jit(_where)/select_n | solution.py:136
  43.8 3.8 %all-gather.2.cloned.1.call-done = bf16[512,1152]{1,0:T(8,128)(2,1)} async-done(((bf16[256,1152]{1,0:T(8,128)(2,1)}), bf16[512,1152]{1,0:T(8,128)(2,1)}) %all-gather.2.cloned.1.call-update) | async-done | bytes 1179664 | tf_op jit(solution)/shard_map/all_gather | solution.py:81
  47.5 2.4 %copy.42 = bf16[512,1152]{0,1:T(8,128)(2,1)} copy(bf16[512,1152]{1,0:T(8,128)(2,1)} %all-gather.2.cloned.1.call-done) | data formatting | bytes 2359296 | tf_op jit(solution)/shard_map/all_gather | solution.py:81
  49.9 8.7 %fusion = (bf16[16,512]{1,0:T(8,128)(2,1)}, f32[16,512,384]{1,2,0:T(8,128)}) fusion(bf16[512,16,72]{0,2,1:T(8,128)(2,1)} %bitcast.53, f32[384,16,72]{0,2,1:T(8,128)S(1)} %bitcast.45, f32[72]{0:T(128)S(1)} %copy-done.7, f32[384,16]{0,1:T(8,128)S(1)} %add_sqrt_fusion), kind=kOutput, calls=%fused_computation.6 | convolution fusion | flops 460595200 | bytes 15573280 | tf_op jit(solution)/shard_map/while/body/eval_jaxpr/qhd,khd->hqk/dot_general | solution.py:44
  58.9 8.5 %fusion.6 = bf16[16,72,512]{2,1,0:T(8,128)(2,1)} fusion(f32[16,512,384]{1,2,0:T(8,128)} %get-tuple-element.30, bf16[384,16,72]{2,1,0:T(8,128)(2,1)} %broadcast_select_fusion), kind=kOutput, calls=%fused_computation.15 | convolution fusion | flops 459866112 | bytes 14647296 | tf_op jit(solution)/shard_map/while/body/eval_jaxpr/hqk,khd->qhd/dot_general | solution.py:49
  67.4 1.3 %reduce-scatter.5.cloned.1.call-done = bf16[256,16]{0,1:T(8,128)(2,1)} async-done(((bf16[512,16]{0,1:T(8,128)(2,1)}), bf16[256,16]{0,1:T(8,128)(2,1)}) %reduce-scatter.5.cloned.1.call-update) | async-done | bytes 8208 | tf_op jit(solution)/shard_map/reduce_scatter | solution.py:87
  68.7 0.7 convert_element_type.86
  69.4 23.4 %reduce-scatter.3.cloned.1.call-done = bf16[256,1152]{0,1:T(8,128)(2,1)} async-done(((bf16[512,1152]{0,1:T(8,128)(2,1)}), bf16[256,1152]{0,1:T(8,128)(2,1)}) %reduce-scatter.3.cloned.1.call-update) | async-done | bytes 589840 | tf_op jit(solution)/shard_map/reduce_scatter | solution.py:84
  92.9 1.2 %fusion.13 = bf16[256,1152]{0,1:T(8,128)(2,1)S(1)} fusion(bf16[256,1152]{0,1:T(8,128)(2,1)} %reduce-scatter.3.cloned.1.call-done, f32[256,16]{0,1:T(8,128)S(1)} %convert_element_type.86), kind=kLoop, calls=%fused_computation.21 | loop fusion | flops 884736 | bytes 1196032 | tf_op jit(solution)/shard_map/convert_element_type | solution.py:92
  94.1 0.3 copy.46
  94.4 0.7 gather_fusion.3
  95.2 1.2 %bitcast_select_fusion = bf16[384,1152]{1,0:T(8,128)(2,1)} fusion(bf16[384,1152]{1,0:T(8,128)(2,1)S(1)} %copy-done.3, bf16[24,16,1152]{2,1,0:T(8,128)(2,1)S(1)} %gather_fusion.3, pred[384]{0:T(512)(128)(4,1)S(1)} %broadcast_in_dim.29), kind=kLoop, calls=%fused_computation.29 | loop fusion | flops 442368 | bytes 2654592 | tf_op jit(solution)/shard_map/jit(_where)/select_n | solution.py:143
  (49 shorter events, 2.6 us)
Async XLA Ops:
  6.5 3.3 %copy-start = (bf16[384,1152]{1,0:T(8,128)(2,1)S(1)}, bf16[384,1152]{1,0:T(8,128)(2,1)}, u32[]{:S(2)}) copy-start(bf16[384,1152]{1,0:T(8,128)(2,1)} %param.10) | copy-start | bytes 2654212
  6.5 4.6 %copy-start.5 = (f32[1152]{0:T(1024)S(1)}, f32[1152]{0:T(1024)}, u32[]{:S(2)}) copy-start(f32[1152]{0:T(1024)} %param.13) | copy-start | bytes 13828
  6.5 4.6 %copy-start.4 = (f32[1152]{0:T(1024)S(1)}, f32[1152]{0:T(1024)}, u32[]{:S(2)}) copy-start(f32[1152]{0:T(1024)} %param.12) | copy-start | bytes 13828
  6.5 41.0 %all-gather.2.cloned.1.call-start = ((), (), s32[]{:S(2)}) async-start(), calls=%async_computation.2 | async-start | bytes 1769472 | tf_op jit(solution)/shard_map/all_gather | solution.py:81
  17.3 1.2 %copy-start.2 = (bf16[256,3456]{1,0:T(8,128)(2,1)}, bf16[256,3456]{1,0:T(8,128)(2,1)S(1)}, u32[]{:S(2)}) copy-start(bf16[256,3456]{1,0:T(8,128)(2,1)S(1)} %convolution_convert_fusion) | copy-start | bytes 5308420
  19.1 0.7 copy-start.6
  21.9 46.8 %reduce-scatter.5.cloned.1.call-start = ((), (), s32[]{:S(2)}) async-start(), calls=%async_computation.4 | async-start | bytes 24576 | tf_op jit(solution)/shard_map/reduce_scatter | solution.py:87
  39.1 1.4 %copy-start.1 = (bf16[384,16,72]{2,1,0:T(8,128)(2,1)S(1)}, bf16[384,16,72]{2,1,0:T(8,128)(2,1)}, u32[]{:S(2)}) copy-start(bf16[384,16,72]{2,1,0:T(8,128)(2,1)} %gather.20) | copy-start | bytes 2654212
  43.8 6.2 %copy-start.7 = (f32[72]{0:T(128)S(1)}, f32[72]{0:T(128)}, u32[]{:S(2)}) copy-start(f32[72]{0:T(128)} %param.15) | copy-start | bytes 868
  58.6 34.2 %reduce-scatter.3.cloned.1.call-start = ((), (), s32[]{:S(2)}) async-start(), calls=%async_computation.3 | async-start | bytes 1769472 | tf_op jit(solution)/shard_map/reduce_scatter | solution.py:84
  94.0 1.2 %copy-start.3 = (bf16[384,1152]{1,0:T(8,128)(2,1)S(1)}, bf16[384,1152]{1,0:T(8,128)(2,1)}, u32[]{:S(2)}) copy-start(bf16[384,1152]{1,0:T(8,128)(2,1)} %param.18) | copy-start | bytes 2654212
Sparse Core Ops, SparseCore 0:
  22.0 25.4 all-gather.1
  58.8 9.9 reduce-scatter.4
  71.0 21.8 reduce-scatter.2
where the time goes:
time: 104 us; the launch traced here: 103 us
  waiting for transfers between devices  28.5 us (27%)
  local copies, waits for them, and re-layouts  23.2 us (22%)
  matrix products  23 us (22%)
  other arithmetic  14.6 us (14%)
  between operations  13.3 us (13%)
    reduce_scatter x1, waiting for transfers between devices, attend(): lax.psum_scatter(numerator.astype(jnp.bfloat16), 'patch', scatter_dimensi...  23.4 us
    dot_general x1, matrix products, partial_terms(): jnp.einsum('qhd,khd->hqk', query_heads, key_heads, preferred_element_type...  8.67 us
    dot_general x1, matrix products, partial_terms(): jnp.einsum('hqk,khd->qhd', weights.astype(jnp.bfloat16), value_heads, pre...  8.54 us
    gather x2, local copies, waits for them, and re-layouts, body(): value_new[position]  6.26 us
    dot_general x1, matrix products, body(): jnp.dot(hidden, projection_weight, preferred_element_type=jnp.float32)  5.78 us
    unnamed x17, local copies, waits for them, and re-layouts  4.56 us
    all_gather x1, waiting for transfers between devices, attend(): every_query = lax.all_gather(queries, 'patch', axis=0, tiled=True)  3.75 us
    select_n x1, other arithmetic, body(): jnp.where(fresh_tile, value_new[position], stale_values.reshape(own_tiles...  3.29 us
  transfers between devices with their start and end apart: 3, of which 3 were waited for; matrix products, arithmetic and copies ran while one was open for 29% of the time, Pallas kernels for 0%

commit v1 on v0

--- a/solution.py
+++ b/solution.py
@@ -7,6 +7,18 @@
 H = 16
 TILE = 16
 epsilon = 1e-06
+
+
+def collect(x, axis, dim):
+    ways, here, lap = (lax.axis_size(axis), lax.axis_index(axis), x.shape[dim])
+    line, have = (x, 1)
+    while have < ways:
+        line = jnp.concatenate(
+            [line, lax.ppermute(line, axis, [(d, (d - have) % ways) for d in range(ways)])],
+            axis=dim,
+        )
+        have = 2 * have
+    return jnp.roll(line, here * lap, axis=dim)
 
 
 def modulate(row_block, shift_term, scale_term):
@@ -78,7 +90,7 @@
 def attend(queries, own_keys, own_values, head_count):
     query_count = queries.shape[0]
     model_width = queries.shape[1]
-    every_query = lax.all_gather(queries, "patch", axis=0, tiled=True)
+    every_query = collect(queries, "patch", 0)
     numerator, totals = own_terms(every_query, own_keys, own_values, head_count, query_count)
     numerator, totals = (
         lax.psum_scatter(

time: 104 us -> 106 us (1.019)
  other arithmetic: 14.6 us -> 20 us
  waiting for transfers between devices: 28.5 us -> 25 us
  starting transfers between devices: 0.27 us -> 3.22 us
  local copies, waits for them, and re-layouts: 23.2 us -> 20.7 us
    all_gather x1 -> x0, waiting for transfers between devices: 3.75 us -> none  [attend(): every_query = lax.all_gather(queries, 'patch', axis=0, tiled=True)]
    concatenate x0 -> x1, other arithmetic: none -> 3.68 us  [collect(): return jnp.roll(line, here * lap, axis=dim)]
    ppermute x0 -> x1, starting transfers between devices: none -> 3 us  [collect(): lax.ppermute(line, axis, [(d, (d - have) % ways) for d in range(ways)])]
    dynamic_slice x0 -> x1, local copies, waits for them, and re-layouts: none -> 2.41 us  [collect(): return jnp.roll(line, here * lap, axis=dim)]
    all_gather x1 -> x0, local copies, waits for them, and re-layouts: 2.39 us -> none  [attend(): every_query = lax.all_gather(queries, 'patch', axis=0, tiled=True)]
    slice x1, local copies, waits for them, and re-layouts: 1.34 us -> 0.09 us  [body(): projected[:, 2 * model_width:].astype(jnp.bfloat16)]
    unnamed x17, local copies, waits for them, and re-layouts: 4.56 us -> 3.34 us
  transfers between devices with their start and end apart: 3 -> 3, of which waited for: 3 -> 2; matrix products, arithmetic and copies ran while one was open for 29% -> 28% of each run, Pallas kernels for 0% -> 0%
where the time goes in v1:
time: 106 us
  waiting for transfers between devices  25 us (24%)
  matrix products  23 us (22%)
  local copies, waits for them, and re-layouts  20.7 us (20%)
  other arithmetic  20 us (19%)
  between operations  13.6 us (13%)
  starting transfers between devices  3.22 us (3%)
    reduce_scatter x1, waiting for transfers between devices, attend(): lax.psum_scatter(numerator.astype(jnp.bfloat16), 'patch', scatter_dimensi...  23.4 us
    dot_general x1, matrix products, partial_terms(): jnp.einsum('qhd,khd->hqk', query_heads, key_heads, preferred_element_type...  8.67 us
    dot_general x1, matrix products, partial_terms(): jnp.einsum('hqk,khd->qhd', weights.astype(jnp.bfloat16), value_heads, pre...  8.53 us
    gather x2, local copies, waits for them, and re-layouts, body(): value_new[position]  6.21 us
    dot_general x1, matrix products, body(): jnp.dot(hidden, projection_weight, preferred_element_type=jnp.float32)  5.78 us
    concatenate x1, other arithmetic, collect(): return jnp.roll(line, here * lap, axis=dim)  3.68 us
    select_n x1, other arithmetic, body(): jnp.where(fresh_tile, value_new[position], stale_values.reshape(own_tiles...  3.53 us
    unnamed x17, local copies, waits for them, and re-layouts  3.34 us
  transfers between devices with their start and end apart: 3, of which 2 were waited for; matrix products, arithmetic and copies ran while one was open for 28% of the time, Pallas kernels for 0%

profile of v1, /device:TPU:0, one launch (start us, length us, event | category | flops | bytes accessed | tf_op | source)
XLA Modules:
  0.0 105.5 jit_solution(1337657164635652284)
XLA Ops:
  6.6 0.8 reshape.206
  7.4 0.6 fusion.28
  8.3 0.7 scatter_custom_fusion
  9.1 0.8 fusion.27
  9.9 0.6 gather_fusion
  11.5 5.8 %convolution_convert_fusion = bf16[256,3456]{1,0:T(8,128)(2,1)S(1)} fusion(bf16[256,1152]{1,0:T(8,128)(2,1)S(1)} %fusion.20, bf16[1152,3456]{1,0:T(8,128)(2,1)} %param.11), kind=kOutput, calls=%fused_computation.10 | convolution fusion | flops 2039316480 | bytes 10321920 | tf_op jit(solution)/shard_map/dot_general | solution.py:133
  17.3 1.2 %copy-done.1 = bf16[256,3456]{1,0:T(8,128)(2,1)} copy-done((bf16[256,3456]{1,0:T(8,128)(2,1)}, bf16[256,3456]{1,0:T(8,128)(2,1)S(1)}, u32[]{:S(2)}) %copy-start.1) | copy-done | bytes 1769496
  18.6 0.4 copy.39
  19.2 0.4 copy.40
  19.8 2.2 %fusion.12 = bf16[256,1152]{1,0:T(8,128)(2,1)} fusion(f32[256,1152]{1,0:T(8,128)S(1)} %copy.40, f32[1152]{0:T(1024)S(1)} %mul.57, bf16[256,3456]{1,0:T(8,128)(2,1)} %copy-done.1), kind=kLoop, calls=%fused_computation.23 | loop fusion | flops 1179648 | bytes 2363904 | tf_op jit(solution)/shard_map/convert_element_type | solution.py:35
  22.0 3.0 %collective-permute-start = (bf16[256,1152]{1,0:T(8,128)(2,1)}, bf16[256,1152]{1,0:T(8,128)(2,1)}, u32[]{:S(2)}, u32[]{:S(2)}) collective-permute-start(bf16[256,1152]{1,0:T(8,128)(2,1)} %fusion.12), channel_id=1, source_target_pairs={{0,1},{1,0},{2,3},{3,2},{4,5},{5,4},{6,7},{7,6},{8,9},{9,8},{10,11... | collective-permute-start | bytes 1769480 | tf_op jit(solution)/shard_map/ppermute | solution.py:17
  25.5 0.7 gather_fusion.2
  26.2 2.6 %fusion.22 = f32[384,1152]{1,0:T(8,128)} fusion(bf16[384,1152]{1,0:T(8,128)(2,1)} %param.16, bf16[24,16,1152]{2,1,0:T(8,128)(2,1)S(1)} %gather_fusion.2, pred[384]{0:T(512)(128)(4,1)S(1)} %broadcast_in_dim.29), kind=kLoop, calls=%fused_computation.38 | loop fusion | flops 884736 | bytes 3539328 | tf_op jit(solution)/shard_map/reshape | solution.py:33
  28.7 2.2 %copy.42 = f32[384,1152]{0,1:T(8,128)S(1)} copy(f32[384,1152]{1,0:T(8,128)} %fusion.22) | data formatting | bytes 3538944 | tf_op jit(solution)/shard_map/reshape | solution.py:33
  30.9 0.8 multiply_reduce_fusion
  31.7 1.6 %gather_fusion.1 = bf16[24,16,1152]{2,1,0:T(8,128)(2,1)} fusion(bf16[16,16,1152]{2,1,0:T(8,128)(2,1)S(1)} %bitcast.50, s32[1024]{0:T(1024)S(1)} %pad_clamp_fusion), kind=kCustom, calls=%fused_computation.1 | custom fusion | bytes 1769568 | tf_op jit(solution)/shard_map/gather | solution.py:149
  33.3 4.6 %gather.20 = bf16[384,16,72]{2,1,0:T(8,128)(2,1)} reshape(bf16[24,16,1152]{2,1,0:T(8,128)(2,1)} %gather_fusion.1) | data formatting | bytes 1769472 | tf_op jit(solution)/shard_map/gather | solution.py:149
  37.9 1.7 %copy.37 = bf16[384,1152]{0,1:T(8,128)(2,1)S(1)} copy(bf16[384,1152]{1,0:T(8,128)(2,1)} %param.17) | data formatting | bytes 1769472 | tf_op args[7]
  39.7 1.9 %copy.38 = bf16[384,16,72]{2,1,0:T(8,128)(2,1)} copy(bf16[384,16,72]{0,2,1:T(8,128)(2,1)S(1)} %bitcast.52) | data formatting | bytes 1769472 | tf_op jit(solution)/shard_map/reshape | solution.py:149
  41.6 0.7 add_sqrt_fusion
  42.4 3.5 %broadcast_select_fusion = bf16[384,16,72]{2,1,0:T(8,128)(2,1)} fusion(bf16[384,16,72]{2,1,0:T(8,128)(2,1)} %gather.20, bf16[384,16,72]{2,1,0:T(8,128)(2,1)} %copy.38, pred[384]{0:T(512)(128)(4,1)S(1)} %broadcast_in_dim.29), kind=kLoop, calls=%fused_computation.18 | loop fusion | flops 442368 | bytes 2654592 | tf_op jit(solution)/shard_map/jit(_where)/select_n | solution.py:148
  45.9 3.7 %fusion.15 = bf16[512,1152]{1,0:T(8,128)(2,1)} fusion(s32[]{:T(128)S(6)} %select_n.97, bf16[256,1152]{1,0:T(8,128)(2,1)} %fusion.12, bf16[256,1152]{1,0:T(8,128)(2,1)} %collective-permute-done), kind=kLoop, calls=%fused_computation.26 | loop fusion | flops 4718592 | bytes 2359300 | tf_op jit(solution)/shard_map/jit(_roll_dynamic)/concatenate | solution.py:21
  49.6 2.4 %copy.41 = bf16[512,1152]{0,1:T(8,128)(2,1)} copy(bf16[512,1152]{1,0:T(8,128)(2,1)} %fusion.15) | data formatting | bytes 2359296 | tf_op jit(solution)/shard_map/jit(_roll_dynamic)/dynamic_slice | solution.py:21
  52.0 8.7 %fusion = (bf16[16,512]{1,0:T(8,128)(2,1)}, f32[16,512,384]{1,2,0:T(8,128)}) fusion(bf16[512,16,72]{0,2,1:T(8,128)(2,1)} %bitcast.53, f32[384,16,72]{0,2,1:T(8,128)S(1)} %bitcast.45, f32[72]{0:T(128)S(1)} %copy-done.7, f32[384,16]{0,1:T(8,128)S(1)} %add_sqrt_fusion), kind=kOutput, calls=%fused_computation.6 | convolution fusion | flops 460595200 | bytes 15573280 | tf_op jit(solution)/shard_map/while/body/eval_jaxpr/qhd,khd->hqk/dot_general | solution.py:56
  60.9 8.5 %fusion.6 = bf16[16,72,512]{2,1,0:T(8,128)(2,1)} fusion(f32[16,512,384]{1,2,0:T(8,128)} %get-tuple-element.30, bf16[384,16,72]{2,1,0:T(8,128)(2,1)} %broadcast_select_fusion), kind=kOutput, calls=%fused_computation.19 | convolution fusion | flops 459866112 | bytes 14647296 | tf_op jit(solution)/shard_map/while/body/eval_jaxpr/hqk,khd->qhd/dot_general | solution.py:61
  69.5 1.6 %reduce-scatter.5.cloned.1.call-done = bf16[256,16]{0,1:T(8,128)(2,1)} async-done(((bf16[512,16]{0,1:T(8,128)(2,1)}), bf16[256,16]{0,1:T(8,128)(2,1)}) %reduce-scatter.5.cloned.1.call-update) | async-done | bytes 8208 | tf_op jit(solution)/shard_map/reduce_scatter | solution.py:99
  71.1 0.7 convert_element_type.86
  71.8 23.4 %reduce-scatter.3.cloned.1.call-done = bf16[256,1152]{0,1:T(8,128)(2,1)} async-done(((bf16[512,1152]{0,1:T(8,128)(2,1)}), bf16[256,1152]{0,1:T(8,128)(2,1)}) %reduce-scatter.3.cloned.1.call-update) | async-done | bytes 589840 | tf_op jit(solution)/shard_map/reduce_scatter | solution.py:96
  95.2 1.2 %fusion.16 = bf16[256,1152]{0,1:T(8,128)(2,1)S(1)} fusion(bf16[256,1152]{0,1:T(8,128)(2,1)} %reduce-scatter.3.cloned.1.call-done, f32[256,16]{0,1:T(8,128)S(1)} %convert_element_type.86), kind=kLoop, calls=%fused_computation.28 | loop fusion | flops 884736 | bytes 1196032 | tf_op jit(solution)/shard_map/convert_element_type | solution.py:104
  96.4 0.3 copy.45
  96.7 0.7 gather_fusion.3
  97.5 1.2 %bitcast_select_fusion = bf16[384,1152]{1,0:T(8,128)(2,1)} fusion(bf16[384,1152]{1,0:T(8,128)(2,1)S(1)} %copy-done.3, bf16[24,16,1152]{2,1,0:T(8,128)(2,1)S(1)} %gather_fusion.3, pred[384]{0:T(512)(128)(4,1)S(1)} %broadcast_in_dim.29), kind=kLoop, calls=%fused_computation.36 | loop fusion | flops 442368 | bytes 2654592 | tf_op jit(solution)/shard_map/jit(_where)/select_n | solution.py:155
  (49 shorter events, 2.7 us)
Async XLA Ops:
  6.5 3.3 %copy-start = (bf16[384,1152]{1,0:T(8,128)(2,1)S(1)}, bf16[384,1152]{1,0:T(8,128)(2,1)}, u32[]{:S(2)}) copy-start(bf16[384,1152]{1,0:T(8,128)(2,1)} %param.10) | copy-start | bytes 2654212
  6.5 4.6 %copy-start.5 = (f32[1152]{0:T(1024)S(1)}, f32[1152]{0:T(1024)}, u32[]{:S(2)}) copy-start(f32[1152]{0:T(1024)} %param.13) | copy-start | bytes 13828
  6.5 4.6 %copy-start.4 = (f32[1152]{0:T(1024)S(1)}, f32[1152]{0:T(1024)}, u32[]{:S(2)}) copy-start(f32[1152]{0:T(1024)} %param.12) | copy-start | bytes 13828
  6.5 64.5 %reduce-scatter.5.cloned.1.call-start = ((), (), s32[]{:S(2)}) async-start(), calls=%async_computation.3 | async-start | bytes 24576 | tf_op jit(solution)/shard_map/reduce_scatter | solution.py:99
  17.3 1.2 %copy-start.1 = (bf16[256,3456]{1,0:T(8,128)(2,1)}, bf16[256,3456]{1,0:T(8,128)(2,1)S(1)}, u32[]{:S(2)}) copy-start(bf16[256,3456]{1,0:T(8,128)(2,1)S(1)} %convolution_convert_fusion) | copy-start | bytes 5308420
  19.1 0.7 copy-start.6
  19.8 5.2 %copy-start.2 = (bf16[256,3456]{1,0:T(8,128)(2,1)S(1)}, bf16[256,3456]{1,0:T(8,128)(2,1)}, u32[]{:S(2)}) copy-start(bf16[256,3456]{1,0:T(8,128)(2,1)} %copy-done.1) | copy-start | bytes 5308420
  22.0 23.9 %collective-permute-start = (bf16[256,1152]{1,0:T(8,128)(2,1)}, bf16[256,1152]{1,0:T(8,128)(2,1)}, u32[]{:S(2)}, u32[]{:S(2)}) collective-permute-start(bf16[256,1152]{1,0:T(8,128)(2,1)} %fusion.12), channel_id=1, source_target_pairs={{0,1},{1,0},{2,3},{3,2},{4,5},{5,4},{6,7},{7,6},{8,9},{9,8},{10,11... | collective-permute-start | bytes 1769480 | tf_op jit(solution)/shard_map/ppermute | solution.py:17
  49.6 2.4 %copy-start.7 = (f32[72]{0:T(128)S(1)}, f32[72]{0:T(128)}, u32[]{:S(2)}) copy-start(f32[72]{0:T(128)} %param.15) | copy-start | bytes 868
  60.7 34.5 %reduce-scatter.3.cloned.1.call-start = ((), (), s32[]{:S(2)}) async-start(), calls=%async_computation.2 | async-start | bytes 1769472 | tf_op jit(solution)/shard_map/reduce_scatter | solution.py:96
  96.4 1.2 %copy-start.3 = (bf16[384,1152]{1,0:T(8,128)(2,1)S(1)}, bf16[384,1152]{1,0:T(8,128)(2,1)}, u32[]{:S(2)}) copy-start(bf16[384,1152]{1,0:T(8,128)(2,1)} %param.18) | copy-start | bytes 2654212
Sparse Core Ops, SparseCore 0:
  60.8 10.2 reduce-scatter.4
  73.3 21.8 reduce-scatter.2
